TPU v7x, 512 devices: a whole 4x4x16 slice. The times are simulated.
512 devices in a mesh: ctx: 64 (over x, z_lo, y), dp: 8 (over z_hi, core).
Axes of the slice: x: 4, y: 4, z: 16 (z_hi: 4, z_lo: 4; z = z_hi * 4 + z_lo), core: 2. Of those that a mesh axis runs over, the one named last changes fastest.
Arguments:
- layer_input: bfloat16 [16, 4096, 4096], P('dp', 'ctx'), may hold values from -1 to 1
- queries: bfloat16 [16, 4096, 1024], P('dp', 'ctx'), may hold values from -8 to 8
- key_states: bfloat16 [16, 4096, 128], P('dp', 'ctx'), may hold values from -8 to 8
- value_states: bfloat16 [16, 4096, 128], P('dp', 'ctx'), may hold values from -6 to 6
- attn_output: bfloat16 [16, 4096, 1024], P('dp', 'ctx'), may hold values from -6 to 6
- out_grad: bfloat16 [16, 4096, 1024], P('dp', 'ctx'), may hold values from -6 to 6
- doc_ids: int32 [16, 4096], P('dp'), may hold values from 0 to 15, never falling along the last dimension, each value on 1 to 1024 neighbouring positions
- positions: int32 [16, 4096], P('dp'), may hold values from 0 to 4095, as said below
Outputs:
- query_grad: bfloat16 [16, 4096, 1024], P('dp', 'ctx')
- kv_weight_grad: float32 [4096, 256], P('ctx')
Inputs may be any that keep to these rules, and one draw needn't show every extreme that they name: `positions`: stored row c * 64 + r of a sequence (c below 64, r below 64) holds a position from r * (64) to (r + 1) * 64 - 1; every position of a sequence is held by exactly one row.
All inputs are finite; a program needn't handle non-finite values.
Results may differ from a plain program's by a relative error of at most 0.005.
Values may be sent and summed in bfloat16 or wider, within the bound.
No kernel may reach another device: no remote copies, remote signals or barrier semaphores. Data moves between devices by JAX's collectives and lax.ppermute only.
A program may use at most 64 MiB of HBM per device.

v0:
```python
import math
import jax
import jax.numpy as jnp
from jax import lax
from jax.sharding import PartitionSpec as P

NEG_FILL = -1e30


def passed_along(x, axis, by):
    length = lax.axis_size(axis)
    return lax.ppermute(x, axis, [(i, (i + by) % length) for i in range(length)])


def heads_first(tensor, head_count):
    seq_count, row_count, width_all = tensor.shape
    head_size = width_all // head_count
    split_up = tensor.reshape(seq_count, row_count, head_count, head_size)
    return split_up.transpose(0, 2, 1, 3).reshape(seq_count, head_count * row_count, head_size)


def local(
    layer_input, queries, key_states, value_states, attn_output, out_grad, doc_ids, positions
):
    seq_count, row_count, model_width = layer_input.shape
    head_size = key_states.shape[2]
    head_count = queries.shape[2] // head_size
    ctx_count = lax.axis_size("ctx")
    ctx_index = lax.axis_index("ctx")
    score_scale = 1.0 / math.sqrt(head_size)
    query_n = heads_first(queries, head_count)
    grad_n = heads_first(out_grad, head_count)
    row_product = (out_grad.astype(jnp.float32) * attn_output.astype(jnp.float32)).reshape(
        seq_count, row_count, head_count, head_size
    )
    delta_n = (
        jnp.sum(row_product, axis=3).transpose(0, 2, 1).reshape(seq_count, head_count * row_count)
    )
    doc_full = jnp.take_along_axis(doc_ids, positions, axis=1)
    own_pos = lax.dynamic_slice_in_dim(positions, ctx_index * row_count, row_count, 1)
    own_doc = lax.dynamic_slice_in_dim(doc_full, ctx_index * row_count, row_count, 1)
    query_pos = jnp.tile(own_pos, (1, head_count))
    query_doc = jnp.tile(own_doc, (1, head_count))
    key_all, value_all = (
        lax.all_gather(key_states, "ctx", axis=1, tiled=True),
        lax.all_gather(value_states, "ctx", axis=1, tiled=True),
    )
    group_rows = 4 * row_count
    query_total = head_count * row_count

    def live_mask(key_doc, key_pos):
        return (key_doc[:, :, None] == query_doc[:, None, :]) & (
            key_pos[:, :, None] <= query_pos[:, None, :]
        )

    def scores_of(key_block):
        return (
            jnp.einsum("skd,snd->skn", key_block, query_n, preferred_element_type=jnp.float32)
            * score_scale
        )

    def stats_step(group_index, loop_state):
        run_max, run_sum = loop_state
        row_start = group_index * group_rows
        key_block = lax.dynamic_slice_in_dim(key_all, row_start, group_rows, 1)
        key_doc = lax.dynamic_slice_in_dim(doc_full, row_start, group_rows, 1)
        key_pos = lax.dynamic_slice_in_dim(positions, row_start, group_rows, 1)
        live_pairs = live_mask(key_doc, key_pos)
        scores = scores_of(key_block)
        block_max = jnp.max(jnp.where(live_pairs, scores, NEG_FILL), axis=1)
        new_max = jnp.maximum(run_max, block_max)
        exp_terms = jnp.where(live_pairs, jnp.exp(scores - new_max[:, None, :]), 0.0)
        run_sum = run_sum * jnp.exp(run_max - new_max) + jnp.sum(exp_terms, axis=1)
        return (new_max, run_sum)

    start_max = jnp.full((seq_count, query_total), NEG_FILL, jnp.float32)
    start_sum = jnp.zeros((seq_count, query_total), jnp.float32)
    run_max, run_sum = lax.fori_loop(0, ctx_count // 4, stats_step, (start_max, start_sum))
    log_total = run_max + jnp.log(run_sum)

    def block_terms(row_start, block_rows):
        key_block = lax.dynamic_slice_in_dim(key_all, row_start, block_rows, 1)
        value_block = lax.dynamic_slice_in_dim(value_all, row_start, block_rows, 1)
        key_doc = lax.dynamic_slice_in_dim(doc_full, row_start, block_rows, 1)
        key_pos = lax.dynamic_slice_in_dim(positions, row_start, block_rows, 1)
        live_pairs = live_mask(key_doc, key_pos)
        scores = scores_of(key_block)
        probs = jnp.where(live_pairs, jnp.exp(scores - log_total[:, None, :]), 0.0)
        probs_half = probs.astype(jnp.bfloat16)
        value_grad = jnp.einsum(
            "skn,snd->skd", probs_half, grad_n, preferred_element_type=jnp.float32
        )
        prob_grad = jnp.einsum(
            "skd,snd->skn", value_block, grad_n, preferred_element_type=jnp.float32
        )
        score_grad = (probs * (prob_grad - delta_n[:, None, :])).astype(jnp.bfloat16)
        query_part = jnp.einsum(
            "skn,skd->snd", score_grad, key_block, preferred_element_type=jnp.float32
        )
        key_grad = (
            jnp.einsum("skn,snd->skd", score_grad, query_n, preferred_element_type=jnp.float32)
            * score_scale
        )
        return (jnp.concatenate([key_grad, value_grad], axis=2), query_part)

    start_query = jnp.zeros((seq_count, query_total, head_size), jnp.float32)

    def pass_on(accumulated):
        return passed_along(accumulated, "ctx", 1)

    def one_block(accumulated, query_sum, step_index):
        block_index = (ctx_index - step_index - 1) % ctx_count
        partial_value, query_part = block_terms(block_index * row_count, row_count)
        return (accumulated + partial_value, query_sum + query_part)

    def four_steps(turn_index, loop_state):
        accumulated, query_sum = loop_state
        for inner_step in range(4):
            accumulated, query_sum = one_block(accumulated, query_sum, 4 * turn_index + inner_step)
            accumulated = pass_on(accumulated)
        return (accumulated, query_sum)

    start_accum = jnp.zeros((seq_count, row_count, 2 * head_size), jnp.float32)
    accumulated, query_sum = lax.fori_loop(
        0, ctx_count // 4 - 1, four_steps, (start_accum, start_query)
    )
    for inner_step in range(3):
        accumulated, query_sum = one_block(accumulated, query_sum, ctx_count - 4 + inner_step)
        accumulated = pass_on(accumulated)
    accumulated, query_sum = one_block(accumulated, query_sum, ctx_count - 1)
    query_grad = (query_sum * score_scale).reshape(seq_count, head_count, row_count, head_size)
    query_grad = (
        query_grad.transpose(0, 2, 1, 3)
        .reshape(seq_count, row_count, head_count * head_size)
        .astype(jnp.bfloat16)
    )
    kv_half = accumulated.astype(jnp.bfloat16)
    flat_input = layer_input.reshape(seq_count * row_count, model_width)
    flat_grad = kv_half.reshape(seq_count * row_count, 2 * head_size)
    row_share = lax.psum_scatter(
        lax.dot_general(
            flat_input, flat_grad, (((0,), (0,)), ((), ())), preferred_element_type=jnp.float32
        ),
        "ctx",
        scatter_dimension=0,
        tiled=True,
    )
    weight_grad = lax.psum(row_share, "dp")
    return (query_grad, weight_grad)


def solution(mesh):
    in_specs = (
        P("dp", "ctx", None),
        P("dp", "ctx", None),
        P("dp", "ctx", None),
        P("dp", "ctx", None),
        P("dp", "ctx", None),
        P("dp", "ctx", None),
        P("dp", None),
        P("dp", None),
    )
    out_specs = (P("dp", "ctx", None), P("ctx", None))
    return jax.shard_map(local, mesh=mesh, in_specs=in_specs, out_specs=out_specs, check_vma=False)
```

profile of v0, /device:TPU:1, one launch (start us, length us, event | category | flops | bytes accessed | tf_op | source)
XLA Modules:
  0.0 2075.9 jit_solution(13382836654781288007)
XLA Ops:
  11.6 69.1 %gather_fusion = s32[8192]{0:T(1024)S(1)} fusion(s32[2,4096]{1,0:T(2,128)S(1)} %copy-done.1, s32[8192]{0:T(1024)S(1)} %bitcast.181), kind=kCustom, calls=%fused_computation | custom fusion | bytes 131072 | tf_op jit(solution)/shard_map/jit(take_along_axis)/gather | solution.py:39
  81.1 244.9 %all-gather.3.cloned.1.call-done = bf16[2,4096,128]{2,1,0:T(8,128)(2,1)} async-done(((bf16[2,64,128]{2,1,0:T(8,128)(2,1)}), bf16[2,4096,128]{2,1,0:T(8,128)(2,1)}) %all-gather.3.cloned.1.call-update) | async-done | bytes 2097168 | tf_op jit(solution)/shard_map/all_gather | solution.py:45
  326.0 30.1 %while.36 = (s32[]{:T(128)}, f32[2,512]{1,0:T(2,128)S(1)}, f32[2,512]{1,0:T(2,128)S(1)}, s32[2,4096]{1,0:T(2,128)S(1)}, s32[2,4096]{1,0:T(2,128)S(1)}, /*index=5...) while((s32[]{:T(128)}, f32[2,512]{1,0:T(2,128)S(1)}, ...), condition=%wide.region_3.4_spmd.clone, body=%wide.region_0.3_spmd.clone.sunk | while | flops 70259720 | bytes 2602182 | solution.py:78
  364.2 316.7 %all-gather.5.cloned.1.call-done = bf16[2,4096,128]{2,1,0:T(8,128)(2,1)} async-done(((bf16[2,64,128]{2,1,0:T(8,128)(2,1)}), bf16[2,4096,128]{2,1,0:T(8,128)(2,1)}) %all-gather.5.cloned.1.call-update) | async-done | bytes 2097168 | tf_op jit(solution)/shard_map/all_gather | solution.py:46
  682.7 754.8 %while.37 = (s32[]{:T(128)}, f32[2,64,256]{2,1,0:T(8,128)S(1)}, f32[2,512,128]{2,1,0:T(8,128)S(1)}, s32[]{:T(128)}, s32[2,4096]{1,0:T(2,128)S(1)}, /*index=5*/s3...) while((s32[]{:T(128)}, f32[2,64,256]{2,1,0:T(8,128)S(1)}, ...), condition=%wide.wide.region_6.7_spmd.clone, body=%wide.wide.region_5.6_spmd.clone.sunk | while | flops 339148864 | bytes 17799364 | solution.py:124
  711.2 9.7 collective-permute-done.2
  749.3 9.6 collective-permute-done.1
  761.0 9.6 collective-permute-done.2
  800.3 10.5 collective-permute-done.1
  850.9 9.6 collective-permute-done.1
  862.6 9.6 collective-permute-done.2
  900.6 9.6 collective-permute-done.1
  912.4 9.6 collective-permute-done.2
  950.6 10.3 collective-permute-done.1
  963.0 9.6 collective-permute-done.2
  1001.0 9.6 collective-permute-done.1
  1012.7 9.6 collective-permute-done.2
  1050.7 9.6 collective-permute-done.1
  1062.4 9.6 collective-permute-done.2
  1100.9 9.7 collective-permute-done.1
  1112.8 9.6 collective-permute-done.2
  1150.8 9.6 collective-permute-done.1
  1162.5 9.6 collective-permute-done.2
  1224.9 9.8 collective-permute-done.3
  1251.3 10.3 collective-permute-done.1
  1263.7 10.9 collective-permute-done.2
  1352.7 9.6 collective-permute-done.1
  1402.4 10.5 collective-permute-done.1
  1415.1 10.6 collective-permute-done.2
  1464.2 9.6 collective-permute-done.6
  1485.4 438.7 %reduce-scatter.4.cloned.1.call-done = f32[64,256]{1,0:T(8,128)} async-done(((f32[4096,256]{1,0:T(8,128)}), f32[64,256]{1,0:T(8,128)}) %reduce-scatter.4.cloned.1.call-update) | async-done | bytes 65552
  1927.5 140.3 %all-reduce.2.cloned.1.call-done = f32[64,256]{0,1:T(8,128)} async-done(((f32[64,256]{0,1:T(8,128)}), f32[64,256]{0,1:T(8,128)}) %all-reduce.2.cloned.1.call-update) | async-done | bytes 65552 | tf_op jit(solution)/shard_map/psum | solution.py:148
  (774 shorter events, 601.3 us)
Async XLA Ops:
  7.2 318.8 %all-gather.3.cloned.1.call-start = ((), (), s32[]{:S(2)}) async-start(), calls=%async_computation.1 | async-start | bytes 2129920 | tf_op jit(solution)/shard_map/all_gather | solution.py:45
  7.9 672.9 %all-gather.5.cloned.1.call-start = ((), (), s32[]{:S(2)}) async-start(), calls=%async_computation.2 | async-start | bytes 2129920 | tf_op jit(solution)/shard_map/all_gather | solution.py:46
  8.7 1915.4 %reduce-scatter.4.cloned.1.call-start = ((), (), s32[]{:S(2)}) async-start(), calls=%async_computation.4 | async-start | bytes 4259840
  685.4 11.8 collective-permute-start
  709.1 11.8 collective-permute-start.2
  735.3 11.8 collective-permute-start
  770.7 11.8 collective-permute-start.3
  785.1 13.0 collective-permute-start
  798.2 12.6 collective-permute-start.1
  836.9 11.8 collective-permute-start
  886.6 11.8 collective-permute-start
  922.0 12.0 collective-permute-start.3
  936.6 11.8 collective-permute-start
  948.5 12.4 collective-permute-start.1
  987.0 11.8 collective-permute-start
  1036.7 11.8 collective-permute-start
  1072.1 12.3 collective-permute-start.3
  1087.0 11.8 collective-permute-start
  1098.8 11.9 collective-permute-start.1
  1136.8 11.8 collective-permute-start
  1186.5 11.8 collective-permute-start
  1221.9 12.8 collective-permute-start.3
  1237.3 11.8 collective-permute-start
  1249.2 12.4 collective-permute-start.1
  1261.6 13.0 collective-permute-start.2
  1289.0 11.8 collective-permute-start
  1338.7 11.8 collective-permute-start
  1388.4 11.8 collective-permute-start
  1400.3 12.6 collective-permute-start.1
  1413.0 12.8 collective-permute-start.2
  1438.4 11.9 collective-permute-start.4
  1482.1 585.6 %all-reduce.2.cloned.1.call-start = ((), (), s32[]{:S(2)}) async-start(), calls=%async_computation.3 | async-start | bytes 262144 | tf_op jit(solution)/shard_map/psum | solution.py:148
  (45 other events, 2106.8 us)
Sparse Core Ops, SparseCore 0:
  10.1 315.8 all-gather.2
  328.1 352.7 all-gather.4
  1482.3 441.7 reduce-scatter.3
  1927.1 140.6 all-reduce.1
where the time goes:
time: 2090 us; the launch traced here: 2080 us
  waiting for transfers between devices  1600 us (77%)
  matrix products  243 us (12%)
  starting transfers between devices  121 us (6%)
  local copies, waits for them, and re-layouts  86.8 us (4%)
    ppermute x63, waiting for transfers between devices, passed_along(): lax.ppermute(x, axis, [(i, (i + by) % length) for i in range(length)])  454 us
    unnamed x5, waiting for transfers between devices  440 us
    all_gather x1, waiting for transfers between devices, local(): lax.all_gather(value_states, 'ctx', axis=1, tiled=True)  317 us
    all_gather x1, waiting for transfers between devices, local(): lax.all_gather(key_states, 'ctx', axis=1, tiled=True)  245 us
    psum x1, waiting for transfers between devices, local(): weight_grad = lax.psum(row_share, 'dp')  140 us
    ppermute x63, starting transfers between devices, passed_along(): lax.ppermute(x, axis, [(i, (i + by) % length) for i in range(length)])  121 us
    dot_general x80, matrix products, scores_of(): jnp.einsum('skd,snd->skn', key_block, query_n, preferred_element_type=jnp...  84.8 us
    gather x2, local copies, waits for them, and re-layouts, local(): doc_full = jnp.take_along_axis(doc_ids, positions, axis=1)  69.1 us
  transfers between devices with their start and end apart: 67, of which 53 were waited for; matrix products, arithmetic and copies ran while one was open for 14% of the time, Pallas kernels for 0%

commit v1 on v0

--- a/solution.py
+++ b/solution.py
@@ -22,6 +22,12 @@
 def local(
     layer_input, queries, key_states, value_states, attn_output, out_grad, doc_ids, positions
 ):
+
+    def touch_the_cube(buf):
+        b_next = jnp.stack([buf for _ in range(lax.axis_size("ctx"))])
+        b_now = lax.all_to_all(b_next, "ctx", 0, 0)
+        return jnp.concatenate(b_now, axis=1)
+
     seq_count, row_count, model_width = layer_input.shape
     head_size = key_states.shape[2]
     head_count = queries.shape[2] // head_size
@@ -43,7 +49,7 @@
     query_doc = jnp.tile(own_doc, (1, head_count))
     key_all, value_all = (
         lax.all_gather(key_states, "ctx", axis=1, tiled=True),
-        lax.all_gather(value_states, "ctx", axis=1, tiled=True),
+        touch_the_cube(value_states),
     )
     group_rows = 4 * row_count
     query_total = head_count * row_count

time: 2090 us -> 1810 us (0.87)
  waiting for transfers between devices: 1600 us -> 1270 us
  local copies, waits for them, and re-layouts: 86.8 us -> 122 us
    all_gather x1 -> x0, waiting for transfers between devices: 317 us -> none  [local(): lax.all_gather(value_states, 'ctx', axis=1, tiled=True)]
    unnamed x5 -> x4, waiting for transfers between devices: 440 us -> 438 us
  transfers between devices with their start and end apart: 67 -> 67, of which waited for: 53 -> 51; matrix products, arithmetic and copies ran while one was open for 14% -> 16% of each run, Pallas kernels for 0% -> 0%
where the time goes in v1:
time: 1810 us; the launch traced here: 1790 us
  waiting for transfers between devices  1270 us (70%)
  matrix products  239 us (13%)
  starting transfers between devices  135 us (7%)
  local copies, waits for them, and re-layouts  122 us (7%)
    ppermute x63, waiting for transfers between devices, passed_along(): lax.ppermute(x, axis, [(i, (i + by) % length) for i in range(length)])  459 us
    unnamed x4, waiting for transfers between devices  438 us
    all_gather x1, waiting for transfers between devices, local(): lax.all_gather(key_states, 'ctx', axis=1, tiled=True)  232 us
    psum x1, waiting for transfers between devices, local(): weight_grad = lax.psum(row_share, 'dp')  139 us
    ppermute x63, starting transfers between devices, passed_along(): lax.ppermute(x, axis, [(i, (i + by) % length) for i in range(length)])  122 us
    dot_general x80, matrix products, scores_of(): jnp.einsum('skd,snd->skn', key_block, query_n, preferred_element_type=jnp...  84.7 us
    gather x2, local copies, waits for them, and re-layouts, local(): doc_full = jnp.take_along_axis(doc_ids, positions, axis=1)  69.1 us
    dot_general x64, matrix products, block_terms(): jnp.einsum('skn,skd->snd', score_grad, key_block, preferred_element_type=...  67.1 us
  transfers between devices with their start and end apart: 67, of which 51 were waited for; matrix products, arithmetic and copies ran while one was open for 16% of the time, Pallas kernels for 0%

profile of v1, /device:TPU:1, one launch (start us, length us, event | category | flops | bytes accessed | tf_op | source)
XLA Modules:
  0.0 1794.1 jit_solution(5832463960063256855)
XLA Ops:
  10.5 12.9 all-to-all-start
  24.4 69.1 %gather_fusion = s32[8192]{0:T(1024)S(1)} fusion(s32[2,4096]{1,0:T(2,128)S(1)} %copy-done.1, s32[8192]{0:T(1024)S(1)} %bitcast.186), kind=kCustom, calls=%fused_computation | custom fusion | bytes 131072 | tf_op jit(solution)/shard_map/jit(take_along_axis)/gather | solution.py:45
  95.4 232.3 %all-gather.2.cloned.1.call-done = bf16[2,4096,128]{2,1,0:T(8,128)(2,1)} async-done(((bf16[2,64,128]{2,1,0:T(8,128)(2,1)}), bf16[2,4096,128]{2,1,0:T(8,128)(2,1)}) %all-gather.2.cloned.1.call-update) | async-done | bytes 2097168 | tf_op jit(solution)/shard_map/all_gather | solution.py:51
  327.7 40.7 %while.36 = (s32[]{:T(128)}, f32[2,512]{1,0:T(2,128)S(1)}, f32[2,512]{1,0:T(2,128)S(1)}, s32[2,4096]{1,0:T(2,128)}, s32[2,4096]{1,0:T(2,128)S(1)}, /*index=5*/bf...) while((s32[]{:T(128)}, f32[2,512]{1,0:T(2,128)S(1)}, ...), condition=%wide.region_3.4_spmd.clone, body=%wide.region_0.3_spmd.clone.sunk | while | flops 70259720 | bytes 2602182 | solution.py:84
  379.1 776.3 %while.37 = (s32[]{:T(128)}, f32[2,64,256]{2,1,0:T(8,128)S(1)}, f32[2,512,128]{2,1,0:T(8,128)S(1)}, s32[]{:T(128)}, s32[2,4096]{1,0:T(2,128)}, /*index=5*/s32[2,...) while((s32[]{:T(128)}, f32[2,64,256]{2,1,0:T(8,128)S(1)}, ...), condition=%wide.wide.region_6.7_spmd.clone, body=%wide.wide.region_5.6_spmd.clone.sunk | while | flops 339148864 | bytes 17816800 | solution.py:130
  449.1 9.6 collective-permute-done.1
  460.8 9.6 collective-permute-done.2
  500.1 10.2 collective-permute-done.1
  512.5 11.0 collective-permute-done.2
  553.7 9.6 collective-permute-done.1
  565.4 9.6 collective-permute-done.2
  604.7 9.6 collective-permute-done.1
  616.4 9.6 collective-permute-done.2
  655.7 10.1 collective-permute-done.1
  668.0 11.1 collective-permute-done.2
  709.2 9.6 collective-permute-done.1
  760.2 9.6 collective-permute-done.1
  823.0 11.1 collective-permute-done.2
  864.4 10.1 collective-permute-done.1
  915.9 9.6 collective-permute-done.1
  927.6 9.6 collective-permute-done.2
  966.9 9.6 collective-permute-done.1
  978.6 9.6 collective-permute-done.2
  1018.3 10.3 collective-permute-done.1
  1030.7 10.9 collective-permute-done.2
  1071.3 9.6 collective-permute-done.1
  1083.0 9.6 collective-permute-done.2
  1122.3 9.6 collective-permute-done.1
  1134.0 9.6 collective-permute-done.2
  1183.6 9.6 collective-permute-done.6
  1205.6 437.7 %reduce-scatter.4.cloned.1.call-done = f32[64,256]{1,0:T(8,128)} async-done(((f32[4096,256]{1,0:T(8,128)}), f32[64,256]{1,0:T(8,128)}) %reduce-scatter.4.cloned.1.call-update) | async-done | bytes 65552
  1646.7 139.3 %all-reduce.2.cloned.1.call-done = f32[64,256]{0,1:T(8,128)} async-done(((f32[64,256]{0,1:T(8,128)}), f32[64,256]{0,1:T(8,128)}) %all-reduce.2.cloned.1.call-update) | async-done | bytes 65552 | tf_op jit(solution)/shard_map/psum | solution.py:154
  (805 shorter events, 636.0 us)
Async XLA Ops:
  7.2 320.5 %all-gather.2.cloned.1.call-start = ((), (), s32[]{:S(2)}) async-start(), calls=%async_computation.2 | async-start | bytes 2129920 | tf_op jit(solution)/shard_map/all_gather | solution.py:51
  10.5 365.1 %all-to-all-start = ((bf16[64,2,64,128]{3,2,1,0:T(8,128)(2,1)}), bf16[64,2,64,128]{3,2,1,0:T(8,128)(2,1)}, u32[]{:S(2)}, u32[]{:S(2)}) async-start(bf16[64,2,64,128]{3,2,1,0:T(8,128)(2,1)} %stack.2), calls=%async_computation | async-start | bytes 4194304 | tf_op jit(solution)/shard_map/all_to_all | solution.py:28
  23.5 1619.8 %reduce-scatter.4.cloned.1.call-start = ((), (), s32[]{:S(2)}) async-start(), calls=%async_computation.4 | async-start | bytes 4259840
  383.1 12.8 collective-permute-start
  435.1 11.8 collective-permute-start
  486.1 11.8 collective-permute-start
  498.0 12.3 collective-permute-start.1
  510.4 13.1 collective-permute-start.2
  523.5 12.2 collective-permute-start.3
  539.7 11.8 collective-permute-start
  590.7 11.8 collective-permute-start
  641.7 11.8 collective-permute-start
  653.6 12.2 collective-permute-start.1
  665.8 13.2 collective-permute-start.2
  679.0 12.3 collective-permute-start.3
  695.2 11.8 collective-permute-start
  746.2 11.8 collective-permute-start
  758.1 11.7 collective-permute-start.1
  797.3 11.8 collective-permute-start
  820.9 13.2 collective-permute-start.2
  834.1 12.3 collective-permute-start.3
  850.4 11.8 collective-permute-start
  862.3 12.2 collective-permute-start.1
  901.9 11.8 collective-permute-start
  952.9 11.8 collective-permute-start
  988.3 12.1 collective-permute-start.3
  1004.3 11.8 collective-permute-start
  1016.2 12.4 collective-permute-start.1
  1028.6 13.0 collective-permute-start.2
  1057.3 11.8 collective-permute-start
  1108.3 11.8 collective-permute-start
  1201.6 584.4 %all-reduce.2.cloned.1.call-start = ((), (), s32[]{:S(2)}) async-start(), calls=%async_computation.3 | async-start | bytes 262144 | tf_op jit(solution)/shard_map/psum | solution.py:154
  (60 other events, 1888.0 us)
Sparse Core Ops, SparseCore 0:
  10.1 317.5 all-gather.1
  1201.7 441.5 reduce-scatter.3
  1646.4 139.5 all-reduce.1
